TPU v7x, 32 devices: a whole 2x2x4 slice. The times are simulated.
32 devices in a mesh: pert: 2 (over y), band: 16 (over z, x, core).
Axes of the slice: x: 2, y: 2, z: 4, core: 2. Of those that a mesh axis runs over, the one named last changes fastest.
Arguments:
- response: bfloat16 [1024, 12288], P('pert', 'band'), parts along dimension 0, may hold values from -6 to 6
- orbitals: bfloat16 [512, 12288], P(None, 'band'), may hold values from -6 to 6
- projectors: bfloat16 [2048, 12288], P(None, 'band'), may hold values from -6 to 6
- potential: float32 [12288], P('band'), may hold values from -1 to 1
- perturbing: float32 [24576], P(('pert', 'band')), parts along dimension 0, may hold values from -6 to 6
- energies: float32 [512], replicated, may hold values from -1 to -0.2
- window_start: int32 [512], replicated, may hold values from 0 to 31, as said below
- block_count: int32 [512], replicated, may hold values from 1 to 9, as said below
Outputs:
- updated_response: bfloat16 [1024, 12288], P('pert', 'band'), parts along dimension 0
- residual: bfloat16 [1024, 12288], P('pert', 'band'), parts along dimension 0
There are 2 independent parts, one for each index of `pert`. A program takes and returns all parts, laid end to end along the dimension named above; an argument that names none is the same for every part. Nothing has to cross between parts.
Inputs may be any that keep to these rules, and one draw needn't show every extreme that they name: `window_start`: band n lies in block n // 16. Each band's window contains its own block and starts at most 4 blocks below it. `block_count`: each band's window ends at most 4 blocks above its own block and never past block 31.
All inputs are finite; a program needn't handle non-finite values.
Results may differ from a plain program's by a relative error of at most 0.0041.
Values may be sent and summed in bfloat16 or wider, within the bound.
A program may use at most 128 MiB of HBM per device.

v0:
```python
import math

import jax
import jax.numpy as jnp
from jax import lax
from jax.sharding import PartitionSpec as P

GY = 8
GZ = 16
NBLK = 32


COEFFS = (
    -5369.0 / 1800.0,
    12.0 / 7.0,
    -15.0 / 56.0,
    10.0 / 189.0,
    -1.0 / 112.0,
    2.0 / 1925.0,
    -1.0 / 16632.0,
)
KINETIC = 0.125
STEP_SIZE = 0.3
CONTRACT_CELLS = (((1,), (1,)), ((), ()))


def padded_2(cells, sides, width):
    for axis, dim in sides:
        count = lax.axis_size(axis)
        head = lax.slice_in_dim(cells, 0, width, axis=dim)
        tail = lax.slice_in_dim(cells, cells.shape[dim] - width, cells.shape[dim], axis=dim)
        cells = jnp.concatenate(
            [
                lax.ppermute(tail, axis, [(i, (i + 1) % count) for i in range(count)]),
                cells,
                lax.ppermute(head, axis, [((i + 1) % count, i) for i in range(count)]),
            ],
            axis=dim,
        )
    return cells


def slab_laplacian(padded, depth):
    centre = padded[:, 6 : 6 + depth]
    result = 3.0 * COEFFS[0] * centre
    for offset in range(1, 7):
        result = result + COEFFS[offset] * (
            padded[:, 6 + offset : 6 + offset + depth] + padded[:, 6 - offset : 6 - offset + depth]
        )
    for axis_number in (2, 3):
        for offset in range(1, 7):
            result = result + COEFFS[offset] * (
                jnp.roll(centre, offset, axis_number) + jnp.roll(centre, -offset, axis_number)
            )
    return result


def shards(
    response, orbitals, projectors, potential, perturbing, energies, window_start, block_count
):
    band_rows = response.shape[0]
    local_cells = response.shape[1]
    devices = lax.axis_size("band")
    cells = local_cells * devices
    plane = GY * GZ
    depth = local_cells // plane
    ace_scale = 1.0 / math.sqrt(cells * projectors.shape[0])
    window_scale = 1.0 / math.sqrt(cells * band_rows)
    padded = padded_2(response.reshape(band_rows, depth, plane), (("band", 1),), 6)
    padded_wide = padded.astype(jnp.float32).reshape(band_rows, depth + 12, GY, GZ)
    kinetic = -KINETIC * slab_laplacian(padded_wide, depth).reshape(band_rows, local_cells)
    response_wide = response.astype(jnp.float32)
    picked = response
    share = lax.psum_scatter(
        lax.dot_general(picked, projectors, CONTRACT_CELLS, preferred_element_type=jnp.float32),
        "band",
        scatter_dimension=0,
        tiled=True,
    )
    ace_intersection = lax.all_gather(
        (share * ace_scale).astype(jnp.bfloat16), "band", axis=0, tiled=True
    )
    ace_term = -jnp.dot(ace_intersection, projectors, preferred_element_type=jnp.float32)
    applied = (
        kinetic + potential[None, :] * response_wide + ace_term - energies[:, None] * response_wide
    )
    orbitals_wide = orbitals.astype(jnp.float32)
    unprojected = -(perturbing[None, :] * orbitals_wide) - applied
    unprojected_low = unprojected.astype(jnp.bfloat16)
    picked = unprojected_low
    window_share = lax.psum_scatter(
        lax.dot_general(picked, orbitals, CONTRACT_CELLS, preferred_element_type=jnp.float32),
        "band",
        scatter_dimension=0,
        tiled=True,
    )
    window_intersection = lax.all_gather(
        (window_share * window_scale).astype(jnp.bfloat16), "band", axis=0, tiled=True
    )
    block_ids = jnp.arange(band_rows, dtype=jnp.int32) // (band_rows // NBLK)
    lowest = window_start[:, None]
    highest = window_start[:, None] + block_count[:, None] - 1
    inside = (block_ids[None, :] >= lowest) & (block_ids[None, :] <= highest)
    window_intersection = jnp.where(
        inside, window_intersection, jnp.zeros_like(window_intersection)
    )
    residual_wide = unprojected - jnp.dot(
        window_intersection, orbitals, preferred_element_type=jnp.float32
    )
    updated_response = (response_wide + STEP_SIZE * residual_wide).astype(jnp.bfloat16)
    return (updated_response, residual_wide.astype(jnp.bfloat16))


def solution(mesh):
    in_specs = (
        P("pert", "band"),
        P(None, "band"),
        P(None, "band"),
        P("band"),
        P(("pert", "band")),
        P(),
        P(),
        P(),
    )
    out_specs = (P("pert", "band"), P("pert", "band"))
    return jax.shard_map(shards, mesh=mesh, in_specs=in_specs, out_specs=out_specs, check_vma=False)
```

profile of v0, /device:TPU:1, one launch (start us, length us, event | category | flops | bytes accessed | tf_op | source)
XLA Modules:
  0.0 228.2 jit_solution(8976337017419959127)
XLA Ops:
  7.2 1.8 copy-done
  9.1 5.0 %fusion.69 = f32[512,2048]{1,0:T(8,128)} fusion(bf16[512,768]{1,0:T(8,128)(2,1)} %param.8, bf16[2048,768]{1,0:T(8,128)(2,1)S(1)} %copy-done), kind=kOutput, calls=%fused_computation.98 | convolution fusion | flops 1610612736 | bytes 8126464 | tf_op jit(solution)/shard_map/dot_general | solution.py:75
  14.1 2.3 %copy.10 = bf16[512,768]{0,1:T(8,128)(2,1)} copy(bf16[512,768]{1,0:T(8,128)(2,1)} %param.8) | data formatting | bytes 1572864 | tf_op args[0]
  16.4 2.6 %collective-permute-start = (bf16[512,6,128]{0,2,1:T(8,128)(2,1)}, bf16[512,6,128]{0,2,1:T(8,128)(2,1)S(1)}, u32[]{:S(2)}, u32[]{:S(2)}) collective-permute-start(bf16[512,6,128]{0,2,1:T(8,128)(2,1)} %bitcast.12), channel_id=1, source_target_pairs={{0,1},{1,2},{2,3},{3,4},{4,5},{5,6},{6,7},{7,8},{8,9},{9,10},{10,1... | collective-permute-start | bytes 2359304 | tf_op jit(solution)/shard_map/ppermute | solution.py:34
  19.0 17.7 %collective-permute-done = bf16[512,6,128]{0,2,1:T(8,128)(2,1)S(1)} collective-permute-done((bf16[512,6,128]{0,2,1:T(8,128)(2,1)}, bf16[512,6,128]{0,2,1:T(8,128)(2,1)S(1)}, u32[]{:S(2)}, u32[]{:S(2)}) %collective-permute-start) | collective-permute-done | bytes 786464 | tf_op jit(solution)/shard_map/ppermute | solution.py:34
  36.7 2.4 %collective-permute-done.1 = bf16[512,6,128]{0,2,1:T(8,128)(2,1)S(1)} collective-permute-done((bf16[512,6,128]{0,2,1:T(8,128)(2,1)}, bf16[512,6,128]{0,2,1:T(8,128)(2,1)S(1)}, u32[]{:S(2)}, u32[]{:S(2)}) %collective-permute-start.1) | collective-permute-done | bytes 786464 | tf_op jit(solution)/shard_map/ppermute | solution.py:36
  51.3 1.6 fusion.52
  52.9 1.8 fusion.50
  54.7 32.8 %reduce-scatter.3.cloned.1.call-done = f32[32,2048]{1,0:T(8,128)} async-done(((f32[512,2048]{1,0:T(8,128)}), f32[32,2048]{1,0:T(8,128)}) %reduce-scatter.3.cloned.1.call-update) | async-done | bytes 262160 | tf_op jit(solution)/shard_map/reduce_scatter | solution.py:74
  87.5 1.6 multiply_convert_fusion
  89.2 1.8 fusion.67
  91.0 3.9 %fusion.66 = (f32[512,6,7,16]{0,3,2,1:T(8,128)}, f32[512,6,7,16]{0,3,2,1:T(8,128)}) fusion(f32[512,18,8,16]{0,3,2,1:T(8,128)} %copy-done.1), kind=kLoop, calls=%fused_computation.95 | loop fusion | bytes 5505024 | tf_op jit(solution)/shard_map/jit(_roll_static)/slice | solution.py:53
  96.8 2.0 fusion.57
  98.8 2.0 fusion.59
  100.8 2.0 fusion.61
  102.8 2.0 fusion.63
  104.8 14.2 %fusion.19 = f32[512,6,8,16]{0,3,2,1:T(8,128)} fusion(f32[512,18,8,16]{0,3,2,1:T(8,128)S(1)} %copy-done.2, f32[512,6,7,16]{0,3,2,1:T(8,128)} %get-tuple-element.37, f32[512,6,1,16]{0,3,2,1:T(8,128)} %get-tuple-element.39, f32[512,6,1,16]{0,3,2,1:T(8,128)} %get-tuple-element.38, f32[512,6,7,16]{0,3,2,1:T(8,128)} %get-tuple-element.36, ...), kind=kLoop, calls=%fused_computation.24 | loop fusion | flops 28704768 | bytes 51904512 | tf_op jit(solution)/shard_map/mul | solution.py:71
  119.0 3.0 %copy.12 = f32[512,768]{1,0:T(8,128)} copy(f32[512,768]{0,1:T(8,128)} %bitcast.11) | data formatting | bytes 3145728 | tf_op jit(solution)/shard_map/mul | solution.py:71
  122.0 10.1 %all-gather.2.cloned.1.call-done = bf16[512,2048]{1,0:T(8,128)(2,1)} async-done(((bf16[32,2048]{1,0:T(8,128)(2,1)}), bf16[512,2048]{1,0:T(8,128)(2,1)}) %all-gather.2.cloned.1.call-update) | async-done | bytes 2097168 | tf_op jit(solution)/shard_map/all_gather | solution.py:80
  132.1 3.5 %fusion.70 = f32[512,768]{1,0:T(8,128)S(1)} fusion(bf16[512,2048]{1,0:T(8,128)(2,1)} %all-gather.2.cloned.1.call-done, bf16[2048,768]{1,0:T(8,128)(2,1)S(1)} %copy-done), kind=kOutput, calls=%fused_computation.99 | convolution fusion | flops 1610612736 | bytes 6815744 | tf_op jit(solution)/shard_map/dot_general | solution.py:83
  136.9 1.8 fusion.38
  138.7 54.2 %reduce-scatter.5.cloned.1.call-done = f32[32,512]{1,0:T(8,128)} async-done(((f32[512,512]{1,0:T(8,128)}), f32[32,512]{1,0:T(8,128)}) %reduce-scatter.5.cloned.1.call-update) | async-done | bytes 65552 | tf_op jit(solution)/shard_map/reduce_scatter | solution.py:91
  193.8 23.2 %all_gather.7 = bf16[512,512]{1,0:T(8,128)(2,1)S(1)} all-gather(bf16[32,512]{1,0:T(8,128)(2,1)S(1)} %multiply_convert_fusion.1), channel_id=1, replica_groups=mesh['pert'=2,'band'=16] {'band'}, dimensions={0}, use_global_device_ids=true | all-gather | bytes 557056 | tf_op jit(solution)/shard_map/all_gather | solution.py:97
  217.0 4.7 %fusion.68 = (bf16[512,768]{1,0:T(8,128)(2,1)}, bf16[512,768]{1,0:T(8,128)(2,1)}) fusion(bf16[512,768]{1,0:T(8,128)(2,1)} %param.8, bf16[512,768]{1,0:T(8,128)(2,1)} %param.9, bf16[512,512]{1,0:T(8,128)(2,1)S(1)} %all_gather.7, s32[512]{0:T(512)S(1)} %get-tuple-element.42, s32[512]{0:T(512)S(1)} %get-tuple-element.43, s32[512]{0:T(512)S(1)} %copy-done.11, ...), kind=kOutput, calls=%fused_computation.97 | convolution fusion | flops 409993216 | bytes 6830080 | tf_op jit(solution)/shard_map/dot_general | solution.py:107
  (44 shorter events, 16.3 us)
Async XLA Ops:
  7.2 1.9 copy-start
  7.2 80.3 %reduce-scatter.3.cloned.1.call-start = ((), (), s32[]{:S(2)}) async-start(), calls=%async_computation.2 | async-start | bytes 4456448 | tf_op jit(solution)/shard_map/reduce_scatter | solution.py:74
  14.1 118.1 %all-gather.2.cloned.1.call-start = ((), (), s32[]{:S(2)}) async-start(), calls=%async_computation.3 | async-start | bytes 2228224 | tf_op jit(solution)/shard_map/all_gather | solution.py:80
  16.4 20.3 %collective-permute-start = (bf16[512,6,128]{0,2,1:T(8,128)(2,1)}, bf16[512,6,128]{0,2,1:T(8,128)(2,1)S(1)}, u32[]{:S(2)}, u32[]{:S(2)}) collective-permute-start(bf16[512,6,128]{0,2,1:T(8,128)(2,1)} %bitcast.12), channel_id=1, source_target_pairs={{0,1},{1,2},{2,3},{3,4},{4,5},{5,6},{6,7},{7,8},{8,9},{9,10},{10,1... | collective-permute-start | bytes 2359304 | tf_op jit(solution)/shard_map/ppermute | solution.py:34
  19.0 20.1 %collective-permute-start.1 = (bf16[512,6,128]{0,2,1:T(8,128)(2,1)}, bf16[512,6,128]{0,2,1:T(8,128)(2,1)S(1)}, u32[]{:S(2)}, u32[]{:S(2)}) collective-permute-start(bf16[512,6,128]{0,2,1:T(8,128)(2,1)} %bitcast.13), channel_id=1, source_target_pairs={{1,0},{2,1},{3,2},{4,3},{5,4},{6,5},{7,6},{8,7},{9,8},{10,9},{11,1... | collective-permute-start | bytes 2359304 | tf_op jit(solution)/shard_map/ppermute | solution.py:36
  40.5 12.4 %copy-start.1 = (f32[512,18,8,16]{0,3,2,1:T(8,128)}, f32[512,18,8,16]{0,3,2,1:T(8,128)S(1)}, u32[]{:S(2)}) copy-start(f32[512,18,8,16]{0,3,2,1:T(8,128)S(1)} %maximum_convert_fusion) | copy-start | bytes 14155780
  89.2 103.8 %reduce-scatter.5.cloned.1.call-start = ((), (), s32[]{:S(2)}) async-start(), calls=%async_computation.4 | async-start | bytes 1114112 | tf_op jit(solution)/shard_map/reduce_scatter | solution.py:91
  91.0 3.9 %copy-start.2 = (f32[512,18,8,16]{0,3,2,1:T(8,128)S(1)}, f32[512,18,8,16]{0,3,2,1:T(8,128)}, u32[]{:S(2)}) copy-start(f32[512,18,8,16]{0,3,2,1:T(8,128)} %copy-done.1) | copy-start | bytes 14155780
  122.0 14.8 %copy-start.7 = (f32[768]{0:T(1024)S(1)}, f32[768]{0:T(1024)}, u32[]{:S(2)}) copy-start(f32[768]{0:T(1024)} %param.11) | copy-start | bytes 9220
  122.0 14.8 %copy-start.8 = (f32[768]{0:T(1024)S(1)}, f32[768]{0:T(1024)}, u32[]{:S(2)}) copy-start(f32[768]{0:T(1024)} %param.12) | copy-start | bytes 9220
  122.0 14.8 %copy-start.9 = (f32[512]{0:T(512)S(1)}, f32[512]{0:T(512)}, u32[]{:S(2)}) copy-start(f32[512]{0:T(512)} %param.13) | copy-start | bytes 6148
  132.1 4.7 %copy-start.3 = (f32[512,768]{1,0:T(8,128)S(1)}, f32[512,768]{1,0:T(8,128)}, u32[]{:S(2)}) copy-start(f32[512,768]{1,0:T(8,128)} %copy.12) | copy-start | bytes 4718596
  132.1 4.7 %copy-start.4 = (bf16[512,768]{1,0:T(8,128)(2,1)S(1)}, bf16[512,768]{1,0:T(8,128)(2,1)}, u32[]{:S(2)}) copy-start(bf16[512,768]{1,0:T(8,128)(2,1)} %param.8) | copy-start | bytes 2359300
  132.1 4.8 %copy-start.5 = (bf16[512,768]{1,0:T(8,128)(2,1)S(1)}, bf16[512,768]{1,0:T(8,128)(2,1)}, u32[]{:S(2)}) copy-start(bf16[512,768]{1,0:T(8,128)(2,1)} %param.9) | copy-start | bytes 2359300
  135.7 1.2 copy-start.6
  136.9 1.8 copy-start.10
  136.9 1.8 copy-start.11
Sparse Core Ops, SparseCore 0:
  14.2 73.2 reduce-scatter.2
  89.7 42.4 all-gather.1
  138.8 54.0 reduce-scatter.4
where the time goes:
time: 229 us; the launch traced here: 228 us
  waiting for transfers between devices  117 us (51%)
  local copies, waits for them, and re-layouts  38.1 us (17%)
  blocking collectives  23.2 us (10%)
  other arithmetic  18.2 us (8%)
  matrix products  15 us (7%)
  between operations  13.9 us (6%)
  starting transfers between devices  2.71 us (1%)
    reduce_scatter x1, waiting for transfers between devices, shards(): lax.psum_scatter(lax.dot_general(picked, orbitals, CONTRACT_CELLS, prefer...  54.2 us
    reduce_scatter x1, waiting for transfers between devices, shards(): lax.psum_scatter(lax.dot_general(picked, projectors, CONTRACT_CELLS, pref...  32.8 us
    all_gather x1, blocking collectives, shards(): lax.all_gather((window_share * window_scale).astype(jnp.bfloat16), 'band'...  23.2 us
    slice x14, local copies, waits for them, and re-layouts, slab_laplacian(): jnp.roll(centre, -offset, axis_number)  22.5 us
    ppermute x1, waiting for transfers between devices, padded_2(): lax.ppermute(tail, axis, [(i, (i + 1) % count) for i in range(count)])  17.7 us
    mul x1, other arithmetic, shards(): -KINETIC  14.2 us
    all_gather x1, waiting for transfers between devices, shards(): lax.all_gather((share * ace_scale).astype(jnp.bfloat16), 'band', axis=0,...  10.1 us
    slice x5, local copies, waits for them, and re-layouts, slab_laplacian(): jnp.roll(centre, offset, axis_number)  7.22 us
  transfers between devices with their start and end apart: 5, of which 5 were waited for; matrix products, arithmetic and copies ran while one was open for 22% of the time, Pallas kernels for 0%

commit v1 on v0

--- a/solution.py
+++ b/solution.py
@@ -1,13 +1,18 @@
+import functools
 import math
 
 import jax
 import jax.numpy as jnp
+import numpy as np
 from jax import lax
+from jax.experimental import pallas as pl
+from jax.experimental.pallas import tpu as pltpu
 from jax.sharding import PartitionSpec as P
 
 GY = 8
 GZ = 16
 NBLK = 32
+REACH = 4
 
 
 COEFFS = (
@@ -21,6 +26,13 @@
 )
 KINETIC = 0.125
 STEP_SIZE = 0.3
+HALO = 6
+NT = (((1,), (1,)), ((), ()))
+WIDTH = 256
+ROWS = 32
+ROW_SHARES = 8
+
+
 CONTRACT_CELLS = (((1,), (1,)), ((), ()))
 
 
@@ -55,7 +67,7 @@
     return result
 
 
-def shards(
+def plain_shards(
     response, orbitals, projectors, potential, perturbing, energies, window_start, block_count
 ):
     band_rows = response.shape[0]
@@ -111,7 +123,352 @@
     return (updated_response, residual_wide.astype(jnp.bfloat16))
 
 
+def plane_operator():
+    plane = GY * GZ
+    op = np.zeros((plane, plane), np.float64)
+    for y in range(GY):
+        for z in range(GZ):
+            out = y * GZ + z
+            op[out, out] += 3.0 * COEFFS[0]
+            for k in range(1, HALO + 1):
+                for sign in (-k, k):
+                    op[((y + sign) % GY) * GZ + z, out] += COEFFS[k]
+                    op[y * GZ + (z + sign) % GZ, out] += COEFFS[k]
+    return (KINETIC * op).astype(np.float32)
+
+
+def kernel(
+    count, groups, ace_scale, window_scale,
+    resp, orb, proj, pot, pert, energies, first, blocks, op_hi, op_lo,
+    updated, residual,
+    halo_l, halo_r, unp, low, acc, c_send, c_recv, x_send, x_recv, z_send, z_recv, full,
+    send_sem, recv_sem, halo_send, halo_recv,
+):
+    rows, cells = resp.shape
+    plane = GY * GZ
+    depth = cells // plane
+    half, quarter = rows // 2, rows // 4
+    share = quarter // groups
+    chunks = proj.shape[0] // WIDTH
+
+    me = lax.axis_index("band")
+    core = me % 2
+    across = (me // 2) % 2
+    level = me // 4
+    left, right = (me + count - 1) % count, (me + 1) % count
+    core_peer = me + 1 - 2 * core
+    x_peer = me + 2 - 4 * across
+    z_levels = [(level + k) % groups for k in range(1, groups)]
+    z_peers = [v * 4 + me % 4 for v in z_levels]
+
+    def remote(src, dst, send, recv, device):
+        return pltpu.make_async_remote_copy(
+            src_ref=src, dst_ref=dst, send_sem=send, recv_sem=recv,
+            device_id={"band": device}, device_id_type=pl.DeviceIdType.MESH,
+        )
+
+    partners = [left, right, core_peer, x_peer] + z_peers
+    barrier = pltpu.get_barrier_semaphore()
+    for device in partners:
+        pl.semaphore_signal(
+            barrier, inc=1, device_id={"band": device}, device_id_type=pl.DeviceIdType.MESH
+        )
+    pl.semaphore_wait(barrier, len(partners))
+
+    width = HALO * plane
+    halos = [
+        remote(resp.at[:, cells - width :], halo_l, halo_send.at[0], halo_recv.at[0], right),
+        remote(resp.at[:, :width], halo_r, halo_send.at[1], halo_recv.at[1], left),
+    ]
+
+    core_row = pl.multiple_of(core * half, half)
+    other_row = pl.multiple_of((1 - core) * half, half)
+    x_row = pl.multiple_of(core * half + across * quarter, quarter)
+    own_row = pl.multiple_of(core * half + across * quarter + level * share, share)
+    x_mine = pl.multiple_of(across * quarter, quarter)
+    x_other = pl.multiple_of((1 - across) * quarter, quarter)
+
+    nz = groups - 1
+    copies = {}
+
+    def begin(j, kind, src, dst, device):
+        copy = remote(src, dst, send_sem.at[j, kind], recv_sem.at[j, kind], device)
+        copy.start()
+        copies[j, kind] = copy
+
+    def partial(j, h, row):
+        if j < chunks:
+            return lax.dot_general(
+                resp[pl.ds(row, half), :], proj[j * WIDTH : (j + 1) * WIDTH, :], NT,
+                preferred_element_type=jnp.float32,
+            )
+        return jnp.concatenate(
+            [
+                lax.dot_general(
+                    low[pl.ds(pl.multiple_of(row + g * quarter, quarter), quarter), :],
+                    orb[pl.ds(window(h, g), WIDTH), :], NT,
+                    preferred_element_type=jnp.float32,
+                )
+                for g in range(2)
+            ],
+            axis=0,
+        )
+
+    reach = REACH * (rows // NBLK)
+
+    def window(h, g):
+        start = h * (2 * quarter - reach) if g == 0 else quarter - reach + h * (quarter + reach)
+        return pl.multiple_of(start, reach)
+
+    def stage_0(j):
+        c_send[j] = partial(j, 1 - core, other_row).astype(jnp.bfloat16)
+        begin(j, 0, c_send.at[j], c_recv.at[j], core_peer)
+        acc[j] = partial(j, core, core_row)
+
+    def stage_1(j):
+        copies[j, 0].wait_recv()
+        x_send[j] = (
+            acc[j, pl.ds(x_other, quarter), :]
+            + c_recv[j, pl.ds(x_other, quarter), :].astype(jnp.float32)
+        ).astype(jnp.bfloat16)
+        begin(j, 1, x_send.at[j], x_recv.at[j], x_peer)
+
+    def stage_2(j):
+        copies[j, 1].wait_recv()
+        total = (
+            acc[j, pl.ds(x_mine, quarter), :]
+            + c_recv[j, pl.ds(x_mine, quarter), :].astype(jnp.float32)
+            + x_recv[j].astype(jnp.float32)
+        )
+        acc[j, :quarter, :] = total
+        z_send[j] = total.astype(jnp.bfloat16)
+        for k in range(nz):
+            begin(
+                j, 2 + k,
+                z_send.at[j, pl.ds(pl.multiple_of(z_levels[k] * share, share), share), :],
+                z_recv.at[j, k], z_peers[k],
+            )
+
+    def stage_3(j):
+        total = acc[j, pl.ds(pl.multiple_of(level * share, share), share), :]
+        for k in range(nz):
+            copies[j, 2 + k].wait_recv()
+            total = total + z_recv[j, k].astype(jnp.float32)
+        scale = ace_scale if j < chunks else window_scale
+        full[j, pl.ds(own_row, share), :] = (total * scale).astype(jnp.bfloat16)
+        piece = full.at[j, pl.ds(own_row, share), :]
+        for k in range(nz):
+            begin(j, 2 + nz + k, piece, piece, z_peers[k])
+
+    def stage_4(j):
+        for k in range(nz):
+            copies[j, 2 + nz + k].wait_recv()
+        piece = full.at[j, pl.ds(x_row, quarter), :]
+        begin(j, 2 + 2 * nz, piece, piece, x_peer)
+
+    def stage_5(j):
+        copies[j, 2 + 2 * nz].wait_recv()
+        piece = full.at[j, pl.ds(core_row, half), :]
+        begin(j, 3 + 2 * nz, piece, piece, core_peer)
+
+    def stage_6(j):
+        copies[j, 3 + 2 * nz].wait_recv()
+        if j < chunks:
+            for lo in range(0, cells, WIDTH):
+                unp[:, lo : lo + WIDTH] += jnp.dot(
+                    full[j], proj[j * WIDTH : (j + 1) * WIDTH, lo : lo + WIDTH],
+                    preferred_element_type=jnp.float32,
+                )
+
+    stages = [stage_0, stage_1, stage_2, stage_3, stage_4, stage_5, stage_6]
+
+    def in_plane():
+        for p in range(depth):
+            cut = resp[:, p * plane : (p + 1) * plane]
+            unp[:, p * plane : (p + 1) * plane] = jnp.dot(
+                cut, op_hi[...], preferred_element_type=jnp.float32
+            ) + jnp.dot(cut, op_lo[...], preferred_element_type=jnp.float32)
+
+    columns = {}
+
+    def column(ref):
+        return jnp.broadcast_to(ref[...].astype(jnp.float32), (plane, rows)).T
+
+    def local_terms(begin_row, end_row):
+        @pl.loop(begin_row // ROWS, end_row // ROWS)
+        def _(i):
+            at = pl.ds(pl.multiple_of(i * ROWS, ROWS), ROWS)
+            planes = [
+                resp[at, p * plane : (p + 1) * plane].astype(jnp.float32) for p in range(depth)
+            ]
+            energy = columns["energies"][at, :]
+            for p in range(depth):
+                cut = slice(p * plane, (p + 1) * plane)
+                value = unp[at, cut] + (energy - pot[:, cut]) * planes[p]
+                value = value - pert[:, cut] * orb[at, cut].astype(jnp.float32)
+                for k in range(1, HALO + 1):
+                    for q in (p - k, p + k):
+                        if 0 <= q < depth:
+                            value = value + (KINETIC * COEFFS[k]) * planes[q]
+                unp[at, cut] = value
+
+    def halo_terms():
+        for copy in halos:
+            copy.wait_recv()
+
+        @pl.loop(0, rows // ROWS)
+        def _(i):
+            at = pl.ds(pl.multiple_of(i * ROWS, ROWS), ROWS)
+            before = [
+                halo_l[at, p * plane : (p + 1) * plane].astype(jnp.float32) for p in range(HALO)
+            ]
+            after = [
+                halo_r[at, p * plane : (p + 1) * plane].astype(jnp.float32) for p in range(HALO)
+            ]
+            for p in range(depth):
+                value = None
+                for k in range(1, HALO + 1):
+                    if p - k < 0:
+                        term = (KINETIC * COEFFS[k]) * before[HALO + p - k]
+                        value = term if value is None else value + term
+                    if p + k >= depth:
+                        term = (KINETIC * COEFFS[k]) * after[p + k - depth]
+                        value = term if value is None else value + term
+                if value is not None:
+                    unp[at, p * plane : (p + 1) * plane] += value
+
+    slots = chunks + len(stages) - 1
+    halo_slot = chunks + 3
+    for t in range(slots):
+        if t == 0:
+            stage_0(0)
+            for copy in halos:
+                copy.start()
+            in_plane()
+            acc[chunks, :, :plane] = column(energies)[:half]
+            acc[chunks, :, plane : 2 * plane] = column(energies)[half:]
+            continue
+        for s in range(len(stages) - 1, -1, -1):
+            j = t - s
+            if 0 <= j < chunks:
+                stages[s](j)
+        if 1 <= t <= 2:
+            columns["energies"] = _HalfView(acc, chunks, (t - 1) * half, plane, t - 1)
+            local_terms((t - 1) * half, t * half)
+        if t == halo_slot:
+            halo_terms()
+
+    for lo in range(0, rows, quarter):
+        low[lo : lo + quarter, :] = unp[lo : lo + quarter, :].astype(jnp.bfloat16)
+    for stage in stages:
+        stage(chunks)
+
+    block = rows // NBLK
+    start_col = column(first)
+    end_col = start_col + column(blocks)
+    for g in range(4):
+        at = slice(g * quarter, (g + 1) * quarter)
+        start = (0, quarter - reach, 2 * quarter - reach, rows - WIDTH)[g]
+        lanes = (lax.broadcasted_iota(jnp.int32, (quarter, plane), 1)).astype(jnp.float32)
+        cuts = []
+        for lo in range(0, WIDTH, plane):
+            ids = jnp.floor((lanes + float(start + lo)) * (1.0 / block))
+            inside = (ids >= start_col[at]) & (ids < end_col[at])
+            cuts.append(
+                jnp.where(inside, full[chunks, at, lo : lo + plane].astype(jnp.float32), 0.0)
+            )
+        weights = jnp.concatenate(cuts, axis=1).astype(jnp.bfloat16)
+        for lo in range(0, cells, WIDTH):
+            wide = unp[at, lo : lo + WIDTH] - jnp.dot(
+                weights, orb[start : start + WIDTH, lo : lo + WIDTH],
+                preferred_element_type=jnp.float32,
+            )
+            residual[at, lo : lo + WIDTH] = wide.astype(jnp.bfloat16)
+            updated[at, lo : lo + WIDTH] = (
+                resp[at, lo : lo + WIDTH].astype(jnp.float32) + STEP_SIZE * wide
+            ).astype(jnp.bfloat16)
+
+    for copy in copies.values():
+        copy.wait_send()
+    for copy in halos:
+        copy.wait_send()
+
+
+class _HalfView:
+    def __init__(self, ref, index, offset, plane, part):
+        self.ref, self.index, self.offset, self.plane, self.part = ref, index, offset, plane, part
+
+    def __getitem__(self, key):
+        at = key[0]
+        lo = self.part * self.plane
+        return self.ref[
+            self.index,
+            pl.ds(pl.multiple_of(at.start - self.offset, ROWS), at.size),
+            lo : lo + self.plane,
+        ]
+
+
+def shards(
+    response, orbitals, projectors, potential, perturbing, energies, window_start, block_count
+):
+    rows, local = response.shape
+    count = lax.axis_size("band")
+    cells = local * count
+    groups = count // 4
+    chunks = projectors.shape[0] // WIDTH
+    half, quarter = rows // 2, rows // 4
+    share = quarter // groups
+    kinds = 4 + 2 * (groups - 1)
+    op = plane_operator()
+    op_hi = jnp.asarray(op).astype(jnp.bfloat16)
+    op_lo = (jnp.asarray(op) - op_hi.astype(jnp.float32)).astype(jnp.bfloat16)
+    halo = (rows, HALO * GY * GZ)
+    low = jnp.bfloat16
+    total = chunks + 1
+    vmem = pl.BlockSpec(memory_space=pltpu.VMEM)
+    return pl.pallas_call(
+        functools.partial(
+            kernel, count, groups,
+            1.0 / math.sqrt(cells * projectors.shape[0]), 1.0 / math.sqrt(cells * rows),
+        ),
+        out_shape=(
+            jax.ShapeDtypeStruct(response.shape, low),
+            jax.ShapeDtypeStruct(response.shape, low),
+        ),
+        in_specs=[vmem] * 10,
+        out_specs=(vmem, vmem),
+        scratch_shapes=[
+            pltpu.VMEM(halo, low),
+            pltpu.VMEM(halo, low),
+            pltpu.VMEM((rows, local), jnp.float32),
+            pltpu.VMEM((rows, local), low),
+            pltpu.VMEM((total, half, WIDTH), jnp.float32),
+            pltpu.VMEM((total, half, WIDTH), low),
+            pltpu.VMEM((total, half, WIDTH), low),
+            pltpu.VMEM((total, quarter, WIDTH), low),
+            pltpu.VMEM((total, quarter, WIDTH), low),
+            pltpu.VMEM((total, quarter, WIDTH), low),
+            pltpu.VMEM((total, groups - 1, share, WIDTH), low),
+            pltpu.VMEM((total, rows, WIDTH), low),
+            pltpu.SemaphoreType.DMA((total, kinds)),
+            pltpu.SemaphoreType.DMA((total, kinds)),
+            pltpu.SemaphoreType.DMA((2,)),
+            pltpu.SemaphoreType.DMA((2,)),
+        ],
+        compiler_params=pltpu.CompilerParams(
+            collective_id=0, has_side_effects=True, vmem_limit_bytes=56 * 1024 * 1024
+        ),
+    )(
+        response, orbitals, projectors,
+        potential[None, :], perturbing[None, :],
+        energies[None, :], window_start[None, :], block_count[None, :],
+        op_hi, op_lo,
+    )
+
+
 def solution(mesh):
+    groups = mesh.shape["band"] // 4
+    fits = groups * 4 == mesh.shape["band"] and ROW_SHARES % groups == 0
     in_specs = (
         P("pert", "band"),
         P(None, "band"),
@@ -123,4 +480,4 @@
         P(),
     )
     out_specs = (P("pert", "band"), P("pert", "band"))
-    return jax.shard_map(shards, mesh=mesh, in_specs=in_specs, out_specs=out_specs, check_vma=False)
+    return jax.shard_map(shards if fits else plain_shards, mesh=mesh, in_specs=in_specs, out_specs=out_specs, check_vma=False)

time: 229 us -> 101 us (0.44)
  waiting for transfers between devices: 117 us -> 0 us
  Pallas kernels: 0 us -> 93.3 us
  local copies, waits for them, and re-layouts: 38.1 us -> 6.66 us
  blocking collectives: 23.2 us -> 0 us
  other arithmetic: 18.2 us -> 0 us
  matrix products: 15 us -> 0 us
  between operations: 13.9 us -> 0.64 us
  starting transfers between devices: 2.71 us -> 0 us
    pallas_call x0 -> x1, Pallas kernels: none -> 93.3 us  [shards(): pl.pallas_call(functools.partial(kernel, count, groups, 1.0 / math.sqrt(c...]
    reduce_scatter x2 -> x0, waiting for transfers between devices: 87 us -> none  [the longest x1 54.2 us: shards(): lax.psum_scatter(lax.dot_general(picked, orbitals, CONTRACT_CELLS, prefer...]
    slice x19 -> x0, local copies, waits for them, and re-layouts: 29.7 us -> none  [the longest x14 22.5 us: slab_laplacian(): jnp.roll(centre, -offset, axis_number)]
    all_gather x1 -> x0, blocking collectives: 23.2 us -> none  [shards(): lax.all_gather((window_share * window_scale).astype(jnp.bfloat16), 'band'...]
    ppermute x2 -> x0, waiting for transfers between devices: 20 us -> none  [the longest x1 17.7 us: padded_2(): lax.ppermute(tail, axis, [(i, (i + 1) % count) for i in range(count)])]
    dot_general x4 -> x0, matrix products: 15 us -> none  [the longest x1 4.97 us: shards(): lax.dot_general(picked, projectors, CONTRACT_CELLS, preferred_element_typ...]
    mul x1 -> x0, other arithmetic: 14.2 us -> none  [shards(): -KINETIC]
    all_gather x1 -> x0, waiting for transfers between devices: 10.1 us -> none  [shards(): lax.all_gather((share * ace_scale).astype(jnp.bfloat16), 'band', axis=0,...]
  transfers between devices with their start and end apart: 5 -> 0, of which waited for: 5 -> 0; matrix products, arithmetic and copies ran while one was open for 22% -> 0% of each run, Pallas kernels for 0% -> 0%
where the time goes in v1:
time: 101 us
  Pallas kernels  93.3 us (92%)
  local copies, waits for them, and re-layouts  6.66 us (7%)
    pallas_call x1, Pallas kernels, shards(): pl.pallas_call(functools.partial(kernel, count, groups, 1.0 / math.sqrt(c...  93.3 us
    unnamed x2, local copies, waits for them, and re-layouts  4.13 us

profile of v1, /device:TPU:1, one launch (start us, length us, event | category | flops | bytes accessed | tf_op | source)
XLA Modules:
  0.0 100.6 jit_solution(6509858828753525403)
XLA Ops:
  0.6 1.3 %broadcast_in_dim.15.pot = f32[1,768]{1,0:T(1,128)} reshape(f32[768]{0:T(1024)} %param.12) | data formatting | bytes 6144 | tf_op jit(solution)/shard_map/broadcast_in_dim | solution.py:463
  1.9 1.3 %broadcast_in_dim.16.pert = f32[1,768]{1,0:T(1,128)} reshape(f32[768]{0:T(1024)} %param.13) | data formatting | bytes 6144 | tf_op jit(solution)/shard_map/broadcast_in_dim | solution.py:463
  3.2 93.3 %shard_map.104 = (bf16[512,768]{1,0:T(8,128)(2,1)}, bf16[512,768]{1,0:T(8,128)(2,1)}) custom-call(bf16[512,768]{1,0:T(8,128)(2,1)} %resp.1, bf16[512,768]{1,0:T(8,128)(2,1)} %orb.1, bf16[2048,768]{1,0:T(8,128)(2,1)} %proj.1, f32[1,768]{1,0:T(1,128)} %broadcast_in_dim.15.pot, f32[1,768]{1,0:T(1,128)} %broadcast_in_dim.16.pert, f32[1,512]{1,0:T(1,128)} %bitcast.3, ...), custom_call_target="tpu_custom_call" | custom-call | tf_op jit(solution)/shard_map/pallas_call | solution.py:429
  96.5 2.1 %copy.13 = bf16[512,768]{1,0:T(8,128)(2,1)} copy(bf16[512,768]{1,0:T(8,128)(2,1)} %get-tuple-element.4) | data formatting | bytes 1572864
  98.5 2.1 %copy.14 = bf16[512,768]{1,0:T(8,128)(2,1)} copy(bf16[512,768]{1,0:T(8,128)(2,1)} %get-tuple-element.5) | data formatting | bytes 1572864

commit v2 on v1

--- a/solution.py
+++ b/solution.py
@@ -31,6 +31,7 @@
 WIDTH = 256
 ROWS = 32
 ROW_SHARES = 8
+DELAYS = (0, 1, 3, 5, 7, 9, 10)
 
 
 CONTRACT_CELLS = (((1,), (1,)), ((), ()))
@@ -139,10 +140,10 @@
 
 def kernel(
     count, groups, ace_scale, window_scale,
-    resp, orb, proj, pot, pert, energies, first, blocks, op_hi, op_lo,
-    updated, residual,
-    halo_l, halo_r, unp, low, acc, c_send, c_recv, x_send, x_recv, z_send, z_recv, full,
-    send_sem, recv_sem, halo_send, halo_recv,
+    resp_hbm, orb_hbm, proj_hbm, pot, pert, energies, first, blocks, op_hi, op_lo,
+    unp_hbm, weights,
+    resp, orb, proj, halo_l, halo_r, unp, low, acc, c_send, c_recv, x_send, x_recv, z_send, z_recv, full,
+    send_sem, recv_sem, halo_send, halo_recv, load_sem, unp_sem,
 ):
     rows, cells = resp.shape
     plane = GY * GZ
@@ -167,13 +168,23 @@
             device_id={"band": device}, device_id_type=pl.DeviceIdType.MESH,
         )
 
+    loads = [pltpu.make_async_copy(resp_hbm, resp, load_sem.at[0])]
+    for j in range(chunks):
+        at = pl.ds(j * WIDTH, WIDTH)
+        loads.append(
+            pltpu.make_async_copy(proj_hbm.at[at, :], proj.at[at, :], load_sem.at[1 + j])
+        )
+    loads.append(pltpu.make_async_copy(orb_hbm, orb, load_sem.at[1 + chunks]))
+    for load in loads:
+        load.start()
+
     partners = [left, right, core_peer, x_peer] + z_peers
     barrier = pltpu.get_barrier_semaphore()
     for device in partners:
         pl.semaphore_signal(
             barrier, inc=1, device_id={"band": device}, device_id_type=pl.DeviceIdType.MESH
         )
-    pl.semaphore_wait(barrier, len(partners))
+    loads[0].wait()
 
     width = HALO * plane
     halos = [
@@ -221,7 +232,11 @@
         return pl.multiple_of(start, reach)
 
     def stage_0(j):
+        if j < chunks:
+            loads[1 + j].wait()
         c_send[j] = partial(j, 1 - core, other_row).astype(jnp.bfloat16)
+        if j == 0:
+            pl.semaphore_wait(barrier, len(partners))
         begin(j, 0, c_send.at[j], c_recv.at[j], core_peer)
         acc[j] = partial(j, core, core_row)
 
@@ -304,8 +319,8 @@
             energy = columns["energies"][at, :]
             for p in range(depth):
                 cut = slice(p * plane, (p + 1) * plane)
-                value = unp[at, cut] + (energy - pot[:, cut]) * planes[p]
-                value = value - pert[:, cut] * orb[at, cut].astype(jnp.float32)
+                value = unp[at, cut] + (energy - pot[cut]) * planes[p]
+                value = value - pert[cut] * orb[at, cut].astype(jnp.float32)
                 for k in range(1, HALO + 1):
                     for q in (p - k, p + k):
                         if 0 <= q < depth:
@@ -337,61 +352,77 @@
                 if value is not None:
                     unp[at, p * plane : (p + 1) * plane] += value
 
-    slots = chunks + len(stages) - 1
-    halo_slot = chunks + 3
+    slots = chunks + DELAYS[-1]
+    halo_slot = chunks + DELAYS[3]
     for t in range(slots):
         if t == 0:
             stage_0(0)
-            for copy in halos:
-                copy.start()
             in_plane()
             acc[chunks, :, :plane] = column(energies)[:half]
             acc[chunks, :, plane : 2 * plane] = column(energies)[half:]
             continue
         for s in range(len(stages) - 1, -1, -1):
-            j = t - s
+            j = t - DELAYS[s]
             if 0 <= j < chunks:
                 stages[s](j)
+        if t == 1:
+            loads[1 + chunks].wait()
         if 1 <= t <= 2:
             columns["energies"] = _HalfView(acc, chunks, (t - 1) * half, plane, t - 1)
             local_terms((t - 1) * half, t * half)
+        if t == 3:
+            for copy in halos:
+                copy.start()
         if t == halo_slot:
             halo_terms()
 
+    unp_copy = pltpu.make_async_copy(unp, unp_hbm, unp_sem)
+    unp_copy.start()
     for lo in range(0, rows, quarter):
         low[lo : lo + quarter, :] = unp[lo : lo + quarter, :].astype(jnp.bfloat16)
-    for stage in stages:
+    for stage in stages[:-1]:
         stage(chunks)
 
     block = rows // NBLK
     start_col = column(first)
     end_col = start_col + column(blocks)
+    insides = []
     for g in range(4):
         at = slice(g * quarter, (g + 1) * quarter)
         start = (0, quarter - reach, 2 * quarter - reach, rows - WIDTH)[g]
         lanes = (lax.broadcasted_iota(jnp.int32, (quarter, plane), 1)).astype(jnp.float32)
-        cuts = []
         for lo in range(0, WIDTH, plane):
             ids = jnp.floor((lanes + float(start + lo)) * (1.0 / block))
             inside = (ids >= start_col[at]) & (ids < end_col[at])
-            cuts.append(
-                jnp.where(inside, full[chunks, at, lo : lo + plane].astype(jnp.float32), 0.0)
-            )
-        weights = jnp.concatenate(cuts, axis=1).astype(jnp.bfloat16)
-        for lo in range(0, cells, WIDTH):
-            wide = unp[at, lo : lo + WIDTH] - jnp.dot(
-                weights, orb[start : start + WIDTH, lo : lo + WIDTH],
-                preferred_element_type=jnp.float32,
-            )
-            residual[at, lo : lo + WIDTH] = wide.astype(jnp.bfloat16)
-            updated[at, lo : lo + WIDTH] = (
-                resp[at, lo : lo + WIDTH].astype(jnp.float32) + STEP_SIZE * wide
-            ).astype(jnp.bfloat16)
+            insides.append((at, lo, jnp.where(inside, 1.0, 0.0)))
+    stages[-1](chunks)
+    for at, lo, inside in insides:
+        weights[at, lo : lo + plane] = (
+            full[chunks, at, lo : lo + plane].astype(jnp.float32) * inside
+        ).astype(jnp.bfloat16)
+    unp_copy.wait()
 
     for copy in copies.values():
         copy.wait_send()
     for copy in halos:
         copy.wait_send()
+
+
+def finish(unp, weights, resp, orb, updated, residual):
+    quarter = unp.shape[0]
+    rows, cells = orb.shape
+    reach = REACH * (rows // NBLK)
+    g = pl.program_id(0)
+    start = pl.multiple_of(jnp.clip(g * quarter - reach, 0, rows - WIDTH), reach)
+    for lo in range(0, cells, WIDTH):
+        cut = slice(lo, lo + WIDTH)
+        wide = unp[:, cut] - jnp.dot(
+            weights[...], orb[pl.ds(start, WIDTH), cut], preferred_element_type=jnp.float32
+        )
+        residual[:, cut] = wide.astype(jnp.bfloat16)
+        updated[:, cut] = (
+            resp[:, cut].astype(jnp.float32) + STEP_SIZE * wide
+        ).astype(jnp.bfloat16)
 
 
 class _HalfView:
@@ -426,18 +457,22 @@
     low = jnp.bfloat16
     total = chunks + 1
     vmem = pl.BlockSpec(memory_space=pltpu.VMEM)
-    return pl.pallas_call(
+    hbm = pl.BlockSpec(memory_space=pl.ANY)
+    unprojected, weights = pl.pallas_call(
         functools.partial(
             kernel, count, groups,
             1.0 / math.sqrt(cells * projectors.shape[0]), 1.0 / math.sqrt(cells * rows),
         ),
         out_shape=(
-            jax.ShapeDtypeStruct(response.shape, low),
-            jax.ShapeDtypeStruct(response.shape, low),
+            jax.ShapeDtypeStruct(response.shape, jnp.float32),
+            jax.ShapeDtypeStruct((rows, WIDTH), low),
         ),
-        in_specs=[vmem] * 10,
-        out_specs=(vmem, vmem),
+        in_specs=[hbm] * 3 + [vmem] * 7,
+        out_specs=(hbm, vmem),
         scratch_shapes=[
+            pltpu.VMEM(response.shape, low),
+            pltpu.VMEM(orbitals.shape, low),
+            pltpu.VMEM(projectors.shape, low),
             pltpu.VMEM(halo, low),
             pltpu.VMEM(halo, low),
             pltpu.VMEM((rows, local), jnp.float32),
@@ -454,16 +489,34 @@
             pltpu.SemaphoreType.DMA((total, kinds)),
             pltpu.SemaphoreType.DMA((2,)),
             pltpu.SemaphoreType.DMA((2,)),
+            pltpu.SemaphoreType.DMA((chunks + 2,)),
+            pltpu.SemaphoreType.DMA(()),
         ],
         compiler_params=pltpu.CompilerParams(
             collective_id=0, has_side_effects=True, vmem_limit_bytes=56 * 1024 * 1024
         ),
     )(
         response, orbitals, projectors,
-        potential[None, :], perturbing[None, :],
+        potential, perturbing,
         energies[None, :], window_start[None, :], block_count[None, :],
         op_hi, op_lo,
     )
+    band = pl.BlockSpec((quarter, local), lambda g: (g, 0))
+    return pl.pallas_call(
+        finish,
+        out_shape=(jax.ShapeDtypeStruct(response.shape, low),) * 2,
+        grid=(4,),
+        in_specs=[
+            band,
+            pl.BlockSpec((quarter, WIDTH), lambda g: (g, 0)),
+            band,
+            pl.BlockSpec(orbitals.shape, lambda g: (0, 0)),
+        ],
+        out_specs=(band, band),
+        cost_estimate=pl.CostEstimate(
+            flops=2 * rows * WIDTH * local, bytes_accessed=12 * rows * local, transcendentals=0
+        ),
+    )(unprojected, weights, response, orbitals)
 
 
 def solution(mesh):

time: 101 us -> 80.3 us (0.80)
  Pallas kernels: 93.3 us -> 79.4 us
  local copies, waits for them, and re-layouts: 6.66 us -> 0 us
    pallas_call x1, Pallas kernels: 93.3 us -> 74.9 us  [shards(): pl.pallas_call(functools.partial(kernel, count, groups, 1.0 / math.sqrt(c...]
    pallas_call x0 -> x1, Pallas kernels: none -> 4.49 us  [shards(): pl.pallas_call(finish, out_shape=(jax.ShapeDtypeStruct(response.shape, lo...]
    unnamed x2 -> x0, local copies, waits for them, and re-layouts: 4.13 us -> none
    broadcast_in_dim x2 -> x0, local copies, waits for them, and re-layouts: 2.53 us -> none  [the longest x1 1.27 us: shards(): potential[None, :]]
where the time goes in v2:
time: 80.3 us; the launch traced here: 80.1 us
  Pallas kernels  79.4 us (99%)
    pallas_call x1, Pallas kernels, shards(): pl.pallas_call(functools.partial(kernel, count, groups, 1.0 / math.sqrt(c...  74.9 us
    pallas_call x1, Pallas kernels, shards(): pl.pallas_call(finish, out_shape=(jax.ShapeDtypeStruct(response.shape, lo...  4.49 us

profile of v2, /device:TPU:1, one launch (start us, length us, event | category | flops | bytes accessed | tf_op | source)
XLA Modules:
  0.0 80.1 jit_solution(11303210829457847779)
XLA Ops:
  0.6 74.9 %shard_map.104 = (f32[512,768]{1,0:T(8,128)}, bf16[512,256]{1,0:T(8,128)(2,1)}) custom-call(bf16[512,768]{1,0:T(8,128)(2,1)} %resp.1, bf16[512,768]{1,0:T(8,128)(2,1)} %orb.1, bf16[2048,768]{1,0:T(8,128)(2,1)} %proj_hbm.1, f32[768]{0:T(1024)} %pot.1, f32[768]{0:T(1024)} %pert.1, f32[1,512]{1,0:T(1,128)} %bitcast.3, s32[1,512]{1,0:T(1,128)} %bitcast.4, ...), custom_call_target="tpu_custom_call" | custom-call | tf_op jit(solution)/shard_map/pallas_call | solution.py:461
  75.6 4.5 %shard_map.105 = (bf16[512,768]{1,0:T(8,128)(2,1)}, bf16[512,768]{1,0:T(8,128)(2,1)}) custom-call(f32[512,768]{1,0:T(8,128)} %get-tuple-element.4.unp, bf16[512,256]{1,0:T(8,128)(2,1)} %get-tuple-element.5.weights, bf16[512,768]{1,0:T(8,128)(2,1)} %resp.1, bf16[512,768]{1,0:T(8,128)(2,1)} %orb.1), custom_call_target="tpu_custom_call" | custom-call | flops 201326592 | bytes 4718592 | tf_op jit(solution)/shard_map/pallas_call | solution.py:505

commit v3 on v2

--- a/solution.py
+++ b/solution.py
@@ -31,7 +31,11 @@
 WIDTH = 256
 ROWS = 32
 ROW_SHARES = 8
+PIECE = 128
+ORDER = (0, 1, 2, 3, 4, 5, 6)
 DELAYS = (0, 1, 3, 5, 7, 9, 10)
+HALO_SLOTS = (4, 6)
+FINISH = 768
 
 
 CONTRACT_CELLS = (((1,), (1,)), ((), ()))
@@ -207,6 +211,9 @@
         copy.start()
         copies[j, kind] = copy
 
+    def cols(j):
+        return slice(0, WIDTH if j < chunks else PIECE)
+
     def partial(j, h, row):
         if j < chunks:
             return lax.dot_general(
@@ -217,7 +224,7 @@
             [
                 lax.dot_general(
                     low[pl.ds(pl.multiple_of(row + g * quarter, quarter), quarter), :],
-                    orb[pl.ds(window(h, g), WIDTH), :], NT,
+                    orb[pl.ds(window(h, g) + (j - chunks) * PIECE, PIECE), :], NT,
                     preferred_element_type=jnp.float32,
                 )
                 for g in range(2)
@@ -234,56 +241,60 @@
     def stage_0(j):
         if j < chunks:
             loads[1 + j].wait()
-        c_send[j] = partial(j, 1 - core, other_row).astype(jnp.bfloat16)
+        w = cols(j)
+        c_send[j, :, w] = partial(j, 1 - core, other_row).astype(jnp.bfloat16)
         if j == 0:
             pl.semaphore_wait(barrier, len(partners))
-        begin(j, 0, c_send.at[j], c_recv.at[j], core_peer)
-        acc[j] = partial(j, core, core_row)
+        begin(j, 0, c_send.at[j, :, w], c_recv.at[j, :, w], core_peer)
+        acc[j, :, w] = partial(j, core, core_row)
 
     def stage_1(j):
+        w = cols(j)
         copies[j, 0].wait_recv()
-        x_send[j] = (
-            acc[j, pl.ds(x_other, quarter), :]
-            + c_recv[j, pl.ds(x_other, quarter), :].astype(jnp.float32)
+        x_send[j, :, w] = (
+            acc[j, pl.ds(x_other, quarter), w]
+            + c_recv[j, pl.ds(x_other, quarter), w].astype(jnp.float32)
         ).astype(jnp.bfloat16)
-        begin(j, 1, x_send.at[j], x_recv.at[j], x_peer)
+        begin(j, 1, x_send.at[j, :, w], x_recv.at[j, :, w], x_peer)
 
     def stage_2(j):
+        w = cols(j)
         copies[j, 1].wait_recv()
         total = (
-            acc[j, pl.ds(x_mine, quarter), :]
-            + c_recv[j, pl.ds(x_mine, quarter), :].astype(jnp.float32)
-            + x_recv[j].astype(jnp.float32)
-        )
-        acc[j, :quarter, :] = total
-        z_send[j] = total.astype(jnp.bfloat16)
+            acc[j, pl.ds(x_mine, quarter), w]
+            + c_recv[j, pl.ds(x_mine, quarter), w].astype(jnp.float32)
+            + x_recv[j, :, w].astype(jnp.float32)
+        )
+        acc[j, :quarter, w] = total
+        z_send[j, :, w] = total.astype(jnp.bfloat16)
         for k in range(nz):
             begin(
                 j, 2 + k,
-                z_send.at[j, pl.ds(pl.multiple_of(z_levels[k] * share, share), share), :],
-                z_recv.at[j, k], z_peers[k],
+                z_send.at[j, pl.ds(pl.multiple_of(z_levels[k] * share, share), share), w],
+                z_recv.at[j, k, :, w], z_peers[k],
             )
 
     def stage_3(j):
-        total = acc[j, pl.ds(pl.multiple_of(level * share, share), share), :]
+        w = cols(j)
+        total = acc[j, pl.ds(pl.multiple_of(level * share, share), share), w]
         for k in range(nz):
             copies[j, 2 + k].wait_recv()
-            total = total + z_recv[j, k].astype(jnp.float32)
+            total = total + z_recv[j, k, :, w].astype(jnp.float32)
         scale = ace_scale if j < chunks else window_scale
-        full[j, pl.ds(own_row, share), :] = (total * scale).astype(jnp.bfloat16)
-        piece = full.at[j, pl.ds(own_row, share), :]
+        full[j, pl.ds(own_row, share), w] = (total * scale).astype(jnp.bfloat16)
+        piece = full.at[j, pl.ds(own_row, share), w]
         for k in range(nz):
             begin(j, 2 + nz + k, piece, piece, z_peers[k])
 
     def stage_4(j):
         for k in range(nz):
             copies[j, 2 + nz + k].wait_recv()
-        piece = full.at[j, pl.ds(x_row, quarter), :]
+        piece = full.at[j, pl.ds(x_row, quarter), cols(j)]
         begin(j, 2 + 2 * nz, piece, piece, x_peer)
 
     def stage_5(j):
         copies[j, 2 + 2 * nz].wait_recv()
-        piece = full.at[j, pl.ds(core_row, half), :]
+        piece = full.at[j, pl.ds(core_row, half), cols(j)]
         begin(j, 3 + 2 * nz, piece, piece, core_peer)
 
     def stage_6(j):
@@ -361,7 +372,7 @@
             acc[chunks, :, :plane] = column(energies)[:half]
             acc[chunks, :, plane : 2 * plane] = column(energies)[half:]
             continue
-        for s in range(len(stages) - 1, -1, -1):
+        for s in ORDER:
             j = t - DELAYS[s]
             if 0 <= j < chunks:
                 stages[s](j)
@@ -370,8 +381,8 @@
         if 1 <= t <= 2:
             columns["energies"] = _HalfView(acc, chunks, (t - 1) * half, plane, t - 1)
             local_terms((t - 1) * half, t * half)
-        if t == 3:
-            for copy in halos:
+        for slot, copy in zip(HALO_SLOTS, halos):
+            if t == slot:
                 copy.start()
         if t == halo_slot:
             halo_terms()
@@ -381,7 +392,8 @@
     for lo in range(0, rows, quarter):
         low[lo : lo + quarter, :] = unp[lo : lo + quarter, :].astype(jnp.bfloat16)
     for stage in stages[:-1]:
-        stage(chunks)
+        for j in range(chunks, chunks + WIDTH // PIECE):
+            stage(j)
 
     block = rows // NBLK
     start_col = column(first)
@@ -395,10 +407,11 @@
             ids = jnp.floor((lanes + float(start + lo)) * (1.0 / block))
             inside = (ids >= start_col[at]) & (ids < end_col[at])
             insides.append((at, lo, jnp.where(inside, 1.0, 0.0)))
-    stages[-1](chunks)
+    for j in range(chunks, chunks + WIDTH // PIECE):
+        stages[-1](j)
     for at, lo, inside in insides:
         weights[at, lo : lo + plane] = (
-            full[chunks, at, lo : lo + plane].astype(jnp.float32) * inside
+            full[chunks + lo // PIECE, at, :PIECE].astype(jnp.float32) * inside
         ).astype(jnp.bfloat16)
     unp_copy.wait()
 
@@ -409,20 +422,17 @@
 
 
 def finish(unp, weights, resp, orb, updated, residual):
-    quarter = unp.shape[0]
-    rows, cells = orb.shape
+    rows = orb.shape[0]
+    quarter = rows // 4
     reach = REACH * (rows // NBLK)
-    g = pl.program_id(0)
-    start = pl.multiple_of(jnp.clip(g * quarter - reach, 0, rows - WIDTH), reach)
-    for lo in range(0, cells, WIDTH):
-        cut = slice(lo, lo + WIDTH)
-        wide = unp[:, cut] - jnp.dot(
-            weights[...], orb[pl.ds(start, WIDTH), cut], preferred_element_type=jnp.float32
-        )
-        residual[:, cut] = wide.astype(jnp.bfloat16)
-        updated[:, cut] = (
-            resp[:, cut].astype(jnp.float32) + STEP_SIZE * wide
-        ).astype(jnp.bfloat16)
+    for g in range(4):
+        at = slice(g * quarter, (g + 1) * quarter)
+        start = min(max(g * quarter - reach, 0), rows - WIDTH)
+        wide = unp[at, :] - jnp.dot(
+            weights[at, :], orb[start : start + WIDTH, :], preferred_element_type=jnp.float32
+        )
+        residual[at, :] = wide.astype(jnp.bfloat16)
+        updated[at, :] = (resp[at, :].astype(jnp.float32) + STEP_SIZE * wide).astype(jnp.bfloat16)
 
 
 class _HalfView:
@@ -455,7 +465,7 @@
     op_lo = (jnp.asarray(op) - op_hi.astype(jnp.float32)).astype(jnp.bfloat16)
     halo = (rows, HALO * GY * GZ)
     low = jnp.bfloat16
-    total = chunks + 1
+    total = chunks + WIDTH // PIECE
     vmem = pl.BlockSpec(memory_space=pltpu.VMEM)
     hbm = pl.BlockSpec(memory_space=pl.ANY)
     unprojected, weights = pl.pallas_call(
@@ -501,17 +511,12 @@
         energies[None, :], window_start[None, :], block_count[None, :],
         op_hi, op_lo,
     )
-    band = pl.BlockSpec((quarter, local), lambda g: (g, 0))
+    band = pl.BlockSpec((rows, FINISH), lambda g: (0, g))
     return pl.pallas_call(
         finish,
         out_shape=(jax.ShapeDtypeStruct(response.shape, low),) * 2,
-        grid=(4,),
-        in_specs=[
-            band,
-            pl.BlockSpec((quarter, WIDTH), lambda g: (g, 0)),
-            band,
-            pl.BlockSpec(orbitals.shape, lambda g: (0, 0)),
-        ],
+        grid=(local // FINISH,),
+        in_specs=[band, pl.BlockSpec((rows, WIDTH), lambda g: (0, 0)), band, band],
         out_specs=(band, band),
         cost_estimate=pl.CostEstimate(
             flops=2 * rows * WIDTH * local, bytes_accessed=12 * rows * local, transcendentals=0

time: 80.3 us -> 75.1 us (0.935)
  Pallas kernels: 79.4 us -> 74.2 us
    pallas_call x1, Pallas kernels: 74.9 us -> 70.7 us  [shards(): pl.pallas_call(functools.partial(kernel, count, groups, 1.0 / math.sqrt(c...]
    pallas_call x1, Pallas kernels: 4.49 us -> 3.5 us  [shards(): pl.pallas_call(finish, out_shape=(jax.ShapeDtypeStruct(response.shape, lo...]
where the time goes in v3:
time: 75.1 us; the launch traced here: 74.9 us
  Pallas kernels  74.2 us (99%)
    pallas_call x1, Pallas kernels, shards(): pl.pallas_call(functools.partial(kernel, count, groups, 1.0 / math.sqrt(c...  70.7 us
    pallas_call x1, Pallas kernels, shards(): pl.pallas_call(finish, out_shape=(jax.ShapeDtypeStruct(response.shape, lo...  3.5 us

profile of v3, /device:TPU:1, one launch (start us, length us, event | category | flops | bytes accessed | tf_op | source)
XLA Modules:
  0.0 74.9 jit_solution(3814601453112599893)
XLA Ops:
  0.6 70.7 %shard_map.104 = (f32[512,768]{1,0:T(8,128)}, bf16[512,256]{1,0:T(8,128)(2,1)}) custom-call(bf16[512,768]{1,0:T(8,128)(2,1)} %resp.1, bf16[512,768]{1,0:T(8,128)(2,1)} %orb.1, bf16[2048,768]{1,0:T(8,128)(2,1)} %proj_hbm.1, f32[768]{0:T(1024)} %pot.1, f32[768]{0:T(1024)} %pert.1, f32[1,512]{1,0:T(1,128)} %bitcast.3, s32[1,512]{1,0:T(1,128)} %bitcast.4, ...), custom_call_target="tpu_custom_call" | custom-call | tf_op jit(solution)/shard_map/pallas_call | solution.py:471
  71.4 3.5 %shard_map.105 = (bf16[512,768]{1,0:T(8,128)(2,1)}, bf16[512,768]{1,0:T(8,128)(2,1)}) custom-call(f32[512,768]{1,0:T(8,128)} %get-tuple-element.4.unp, bf16[512,256]{1,0:T(8,128)(2,1)} %get-tuple-element.5.weights, bf16[512,768]{1,0:T(8,128)(2,1)} %resp.1, bf16[512,768]{1,0:T(8,128)(2,1)} %orb.1), custom_call_target="tpu_custom_call" | custom-call | flops 201326592 | bytes 4718592 | tf_op jit(solution)/shard_map/pallas_call | solution.py:515
